TPU v7x, 128 devices: a whole 4x4x4 slice. The times are simulated.
128 devices in a mesh: blk: 8 (over z, core), grp: 16 (over x, y).
Axes of the slice: x: 4, y: 4, z: 4, core: 2. Of those that a mesh axis runs over, the one named last changes fastest.
Arguments:
- user_prior: float32 [32768, 128], P(('blk', 'grp')), may hold values from -6 to 6
- item_factors: bfloat16 [524288, 128], P(('blk', 'grp')), may hold values from -0.375 to 0.375
- user_tiles: int32 [8192], P(('blk', 'grp')), may hold values from 0 to 31
- item_tiles: int32 [8192], P(('blk', 'grp')), may hold values from 0 to 4095, as said below
- counts: int32 [8192, 128, 128], P(('blk', 'grp')), may hold values from 0 to 20, as said below
Outputs:
- user_factors: float32 [32768, 128], P(('blk', 'grp'))
Inputs may be any that keep to these rules, and one draw needn't show every extreme that they name: `item_tiles`: item tile t is held by device t // 32 of blk+grp. The entries of one device name tiles of 32 different holders, exactly 2 entries for each holder that they name, in no particular order. In each device's 64 entries, those whose tile of counts has a nonzero value come before those whose tile is all zero; in every group along grp at least one device has all 64 entries of the first kind.
All inputs are finite; a program needn't handle non-finite values.
Results may differ from a plain program's by a relative error of at most 0.0003.
The roundings to bfloat16 on the way count: a program that leaves them out, or rounds other values in their place, can miss the bound.
Values may be sent and summed in bfloat16 or wider, within the bound.
A program may use at most 128 MiB of HBM per device.

v0:
```python
import jax
import jax.numpy as jnp
from jax import lax
from jax.sharding import PartitionSpec as P

ITERS = 3
ALPHA = 40.0
REG = 32.0
EPS = 1e-06


def fetch_tiles(item_factors, item_tiles, pairs, tile, rank):
    n_all = lax.axis_size(("blk", "grp"))
    tiles_held = item_factors.shape[0] // tile
    slots_each = max(2, pairs // n_all)
    owner = item_tiles // tiles_held
    local_slot = item_tiles % tiles_held
    position = jnp.arange(pairs, dtype=jnp.int32)
    earlier = (owner[None, :] == owner[:, None]) & (position[None, :] < position[:, None])
    order = jnp.sum(earlier.astype(jnp.int32), axis=1)
    requests = jnp.full((n_all, slots_each), -1, jnp.int32).at[owner, order].set(local_slot)
    wanted = lax.all_to_all(requests, ("blk", "grp"), split_axis=0, concat_axis=0, tiled=True)
    held = item_factors.reshape(tiles_held, tile, rank)
    picked = jnp.take(held, jnp.maximum(wanted, 0), axis=0)
    picked = jnp.where((wanted >= 0)[:, :, None, None], picked, jnp.zeros((), picked.dtype))
    arrived = lax.all_to_all(picked, ("blk", "grp"), split_axis=0, concat_axis=0, tiled=True)
    return arrived[owner, order]


def body(user_prior, item_factors, user_tiles, item_tiles, counts):
    pairs = counts.shape[0]
    tile = counts.shape[1]
    rank = item_factors.shape[1]
    n_grp = lax.axis_size("grp")
    own_rows = user_prior.shape[0]
    block_rows = own_rows * n_grp
    user_blocks = block_rows // tile
    span = min(32, pairs)
    gram_local = lax.dot_general(
        item_factors, item_factors, (((0,), (0,)), ((), ())), preferred_element_type=jnp.float32
    )
    gram = lax.psum(gram_local, ("blk", "grp"))
    pair_tiles = fetch_tiles(item_factors, item_tiles, pairs, tile, rank)
    live = jnp.sum(jnp.any(counts > 0, axis=(1, 2)).astype(jnp.int32))
    rounds = (live + span - 1) // span
    tile_ids = jnp.arange(user_blocks, dtype=jnp.int32)

    def accumulate(low_tiles, with_rhs):

        def one_round(index, totals):
            start = index * span
            users = lax.dynamic_slice_in_dim(user_tiles, start, span)
            factors = lax.dynamic_slice_in_dim(pair_tiles, start, span)
            counted = lax.dynamic_slice_in_dim(counts, start, span).astype(jnp.float32)
            selector = (tile_ids[:, None] == users[None, :]).astype(jnp.float32)
            users_low = jnp.take(low_tiles, users, axis=0)
            scores = jnp.einsum(
                "bur,bir->bui", users_low, factors, preferred_element_type=jnp.float32
            )
            scaled = (ALPHA * counted * scores).astype(jnp.bfloat16)
            back = jnp.einsum("bui,bir->bur", scaled, factors, preferred_element_type=jnp.float32)
            result = [
                totals[0]
                + jnp.einsum("tb,bur->tur", selector, back, precision=lax.Precision.HIGHEST)
            ]
            if with_rhs:
                confidence = jnp.where(counted > 0, 1.0 + ALPHA * counted, 0.0).astype(jnp.bfloat16)
                pulled = jnp.einsum(
                    "bui,bir->bur", confidence, factors, preferred_element_type=jnp.float32
                )
                result.append(
                    totals[1]
                    + jnp.einsum("tb,bur->tur", selector, pulled, precision=lax.Precision.HIGHEST)
                )
            return tuple(result)

        zeros = jnp.zeros((user_blocks, tile, rank), jnp.float32)
        start_state = (zeros, zeros) if with_rhs else (zeros,)
        totals = lax.fori_loop(0, rounds, one_round, start_state)
        return tuple((total.reshape(block_rows, rank) for total in totals))

    def gram_term(vectors):
        return jnp.dot(vectors, gram, precision=lax.Precision.HIGHEST) + REG * vectors

    def row_sum(left, right):
        return jnp.sum(left * right, axis=1, keepdims=True)

    whole = lax.all_gather(user_prior, "grp", axis=0, tiled=True)
    pair_part, rhs_part = accumulate(
        whole.astype(jnp.bfloat16).reshape(user_blocks, tile, rank), True
    )
    pair_total, rhs_total = lax.psum((pair_part, rhs_part), "grp")
    solution = whole
    residual = rhs_total - (gram_term(solution) + pair_total)
    direction = residual
    norm_now = row_sum(residual, residual)
    for step in range(ITERS):
        (pair_part,) = accumulate(
            direction.astype(jnp.bfloat16).reshape(user_blocks, tile, rank), False
        )
        image = gram_term(direction) + lax.psum(pair_part, "grp")
        alpha = norm_now / (row_sum(direction, image) + EPS)
        solution = solution + alpha * direction
        residual = residual - alpha * image
        fresh = row_sum(residual, residual)
        direction = residual + fresh / (norm_now + EPS) * direction
        norm_now = fresh
    return lax.dynamic_slice_in_dim(solution, lax.axis_index("grp") * own_rows, own_rows, 0)


def solution(mesh):
    in_specs = (
        P(("blk", "grp"), None),
        P(("blk", "grp"), None),
        P(("blk", "grp")),
        P(("blk", "grp")),
        P(("blk", "grp"), None, None),
    )
    out_specs = P(("blk", "grp"), None)
    return jax.shard_map(body, mesh=mesh, in_specs=in_specs, out_specs=out_specs, check_vma=False)
```

profile of v0, /device:TPU:0, one launch (start us, length us, event | category | flops | bytes accessed | tf_op | source)
XLA Modules:
  0.0 787.2 jit_solution(2010041510047153230)
XLA Ops:
  15.4 20.5 %all_to_all.14 = s32[128,1,2]{2,1,0:T(1,128)S(1)} all-to-all(s32[128,1,2]{2,1,0:T(1,128)S(1)} %copy.108), channel_id=1, replica_groups=mesh['blk'=8,'grp'=16] {'blk','grp'}, dimensions={0} | all-to-all | bytes 2048 | tf_op jit(solution)/shard_map/all_to_all | solution.py:22
  36.5 8.4 %gather_fusion.4 = bf16[256,128,128]{2,1,0:T(8,128)(2,1)} fusion(bf16[32,128,128]{2,1,0:T(8,128)(2,1)S(1)} %bitcast.108, s32[1024]{0:T(1024)S(1)} %pad_clamp_fusion.4), kind=kCustom, calls=%fused_computation.4 | custom fusion | bytes 16778240 | tf_op jit(solution)/shard_map/jit(_take)/gather | solution.py:24
  44.9 7.4 select_select_fusion
  52.3 6.1 all-to-all-start.1
  61.1 104.8 %all-gather.2.cloned.1.call-done = f32[4096,128]{0,1:T(8,128)} async-done(((f32[256,128]{0,1:T(8,128)}), f32[4096,128]{0,1:T(8,128)}) %all-gather.2.cloned.1.call-update) | async-done | bytes 2097168 | tf_op jit(solution)/shard_map/all_gather | solution.py:88
  176.5 18.2 %while.46 = (s32[]{:T(128)}, f32[32,128,128]{2,0,1:T(8,128)}, f32[32,128,128]{2,0,1:T(8,128)}, s32[]{:T(128)}, s32[64]{0:T(128)S(1)}, /*index=5*/s32[64,128,128]...) while((s32[]{:T(128)}, f32[32,128,128]{2,0,1:T(8,128)}, ...), condition=%wide.region_5.7_spmd.clone, body=%wide.region_4.6_spmd.clone.sunk | while | flops 812125440 | bytes 44048128 | solution.py:79
  182.9 6.1 fusion.187
  189.4 5.4 fusion.189
  198.3 4.6 copy.165
  206.3 4.6 copy.166
  211.2 58.5 %all-reduce.7.cloned.1.call-done = f32[128,128]{1,0:T(8,128)} async-done(((f32[128,128]{1,0:T(8,128)}), f32[128,128]{1,0:T(8,128)}) %all-reduce.7.cloned.1.call-update) | async-done | bytes 65552 | tf_op jit(solution)/shard_map/psum | solution.py:42
  269.7 105.7 %all-reduce.15.cloned.1.call-done = (f32[4096,128]{0,1:T(8,128)}, f32[4096,128]{0,1:T(8,128)}) async-done(((f32[4096,128]{0,1:T(8,128)}, f32[4096,128]{0,1:T(8,128)}), (f32[4096,128]{0,1:T(8,128)}, f32[4096,128]{0,1:T(8,128)})) %all-reduce.15.cloned.1.call-update) | async-done | bytes 4194320 | tf_op jit(solution)/shard_map/psum | solution.py:92
  375.5 7.0 fusion.133
  385.4 12.0 %while.47 = (s32[]{:T(128)}, f32[32,128,128]{2,0,1:T(8,128)}, s32[]{:T(128)}, s32[64]{0:T(128)S(1)}, s32[64,128,128]{2,1,0:T(8,128)}, /*index=5*/bf16[32,128,128...) while((s32[]{:T(128)}, f32[32,128,128]{2,0,1:T(8,128)}, ...), condition=%wide.region_11.13_spmd.clone, body=%wide.region_10.12_spmd.clone.sunk | while | flops 472910112 | bytes 15735391 | solution.py:79
  391.5 5.9 fusion.196
  405.9 102.4 %all-reduce.9.cloned.1.call-done = f32[4096,128]{0,1:T(8,128)} async-done(((f32[4096,128]{0,1:T(8,128)}), f32[4096,128]{0,1:T(8,128)}) %all-reduce.9.cloned.1.call-update) | async-done | bytes 2097168 | tf_op jit(solution)/shard_map/psum | solution.py:101
  508.3 5.5 multiply_reduce_fusion.3
  519.1 12.1 %while.48 = (s32[]{:T(128)}, f32[32,128,128]{2,0,1:T(8,128)}, s32[]{:T(128)}, s32[64]{0:T(128)S(1)}, s32[64,128,128]{2,1,0:T(8,128)}, /*index=5*/bf16[32,128,128...) while((s32[]{:T(128)}, f32[32,128,128]{2,0,1:T(8,128)}, ...), condition=%wide.region_16.18_spmd.clone, body=%wide.region_15.17_spmd.clone.sunk | while | flops 472910112 | bytes 15735391 | solution.py:79
  525.3 5.9 fusion.203
  539.5 101.9 %all-reduce.11.cloned.1.call-done = f32[4096,128]{0,1:T(8,128)} async-done(((f32[4096,128]{0,1:T(8,128)}), f32[4096,128]{0,1:T(8,128)}) %all-reduce.11.cloned.1.call-update) | async-done | bytes 2097168 | tf_op jit(solution)/shard_map/psum | solution.py:101
  641.4 5.3 multiply_reduce_fusion.1
  653.1 12.3 %while.49 = (s32[]{:T(128)}, f32[32,128,128]{2,0,1:T(8,128)}, s32[]{:T(128)}, s32[64]{0:T(128)S(1)}, s32[64,128,128]{2,1,0:T(8,128)}, /*index=5*/bf16[32,128,128...) while((s32[]{:T(128)}, f32[32,128,128]{2,0,1:T(8,128)}, ...), condition=%wide.region_21.23_spmd.clone, body=%wide.region_20.22_spmd.clone.sunk | while | flops 472910112 | bytes 15735391 | solution.py:79
  659.3 5.9 fusion.210
  671.3 102.4 %all-reduce.13.cloned.1.call-done = f32[4096,128]{0,1:T(8,128)} async-done(((f32[4096,128]{0,1:T(8,128)}), f32[4096,128]{0,1:T(8,128)}) %all-reduce.13.cloned.1.call-update) | async-done | bytes 2097168 | tf_op jit(solution)/shard_map/psum | solution.py:101
  (109 shorter events, 96.5 us)
Async XLA Ops:
  7.4 29.1 %copy-start = (bf16[4096,128]{1,0:T(8,128)(2,1)S(1)}, bf16[4096,128]{1,0:T(8,128)(2,1)}, u32[]{:S(2)}) copy-start(bf16[4096,128]{1,0:T(8,128)(2,1)} %param.16) | copy-start | bytes 3145732
  7.4 3.5 copy-start.11
  52.3 6.1 copy-start.10
  52.3 116.7 %all-to-all-start.1 = ((bf16[128,2,128,128]{3,2,1,0:T(8,128)(2,1)}), bf16[128,2,128,128]{3,2,1,0:T(8,128)(2,1)}, u32[]{:S(2)}, u32[]{:S(2)}) async-start(bf16[128,2,128,128]{3,2,1,0:T(8,128)(2,1)} %select_select_fusion), calls=%async_computation.1 | async-start | bytes 16777216 | tf_op jit(solution)/shard_map/all_to_all | solution.py:26
  58.4 107.5 %all-gather.2.cloned.1.call-start = ((), (), s32[]{:S(2)}) async-start(), calls=%async_computation.2 | async-start | bytes 2228224 | tf_op jit(solution)/shard_map/all_gather | solution.py:88
  59.2 210.5 %all-reduce.7.cloned.1.call-start = ((), (), s32[]{:S(2)}) async-start(), calls=%async_computation.3 | async-start | bytes 131072 | tf_op jit(solution)/shard_map/psum | solution.py:42
  60.4 315.1 %all-reduce.15.cloned.1.call-start = ((), (), s32[]{:S(2)}) async-start(), calls=%async_computation.7 | async-start | bytes 8388608 | tf_op jit(solution)/shard_map/psum | solution.py:92
  173.3 3.2 copy-start.9
  182.9 6.1 copy-start.2
  210.9 297.3 %all-reduce.9.cloned.1.call-start = ((), (), s32[]{:S(2)}) async-start(), calls=%async_computation.4 | async-start | bytes 4194304 | tf_op jit(solution)/shard_map/psum | solution.py:101
  405.4 102.9 %copy-start.8 = (f32[128,128]{1,0:T(8,128)S(1)}, f32[128,128]{1,0:T(8,128)}, u32[]{:S(2)}) copy-start(f32[128,128]{1,0:T(8,128)} %all-reduce.7.cloned.1.call-done) | copy-start | bytes 196612
  405.4 236.0 %all-reduce.11.cloned.1.call-start = ((), (), s32[]{:S(2)}) async-start(), calls=%async_computation.5 | async-start | bytes 4194304 | tf_op jit(solution)/shard_map/psum | solution.py:101
  508.3 5.5 copy-start.3
  514.2 2.0 copy-start.4
  539.3 234.4 %all-reduce.13.cloned.1.call-start = ((), (), s32[]{:S(2)}) async-start(), calls=%async_computation.6 | async-start | bytes 4194304 | tf_op jit(solution)/shard_map/psum | solution.py:101
  641.4 5.4 copy-start.5
  646.7 1.6 copy-start.6
  671.1 102.6 %copy-start.7 = (f32[4096,128]{0,1:T(8,128)S(1)}, f32[4096,128]{0,1:T(8,128)}, u32[]{:S(2)}) copy-start(f32[4096,128]{0,1:T(8,128)} %get-tuple-element.504) | copy-start | bytes 6291460
  773.7 5.9 copy-start.1
Sparse Core Ops, SparseCore 0:
  61.3 104.5 all-gather.1
  405.5 102.6 all-reduce.8
  671.2 102.3 all-reduce.12
Sparse Core Ops, SparseCore 1:
  64.5 205.2 all-reduce.6
  273.0 102.4 all-reduce.14
  539.3 102.0 all-reduce.10
where the time goes:
time: 795 us; the launch traced here: 787 us
  waiting for transfers between devices  576 us (72%)
  local copies, waits for them, and re-layouts  78.9 us (10%)
  matrix products  69 us (9%)
  blocking collectives  20.5 us (3%)
  other arithmetic  19.5 us (2%)
  between operations  16 us (2%)
    psum x3, waiting for transfers between devices, body(): image = gram_term(direction) + lax.psum(pair_part, 'grp')  307 us
    psum x1, waiting for transfers between devices, body(): pair_total, rhs_total = lax.psum((pair_part, rhs_part), 'grp')  106 us
    all_gather x1, waiting for transfers between devices, body(): whole = lax.all_gather(user_prior, 'grp', axis=0, tiled=True)  105 us
    psum x1, waiting for transfers between devices, body(): gram = lax.psum(gram_local, ('blk', 'grp'))  58.5 us
    unnamed x32, local copies, waits for them, and re-layouts  28.6 us
    dot_general x4, matrix products, one_round(): jnp.einsum('tb,bur->tur', selector, back, precision=lax.Precision.HIGHEST)  23.8 us
    dot_general x4, matrix products, gram_term(): jnp.dot(vectors, gram, precision=lax.Precision.HIGHEST) + REG * vectors  21.8 us
    all_to_all x1, blocking collectives, fetch_tiles(): lax.all_to_all(requests, ('blk', 'grp'), split_axis=0, concat_axis=0, til...  20.5 us
  transfers between devices with their start and end apart: 7, of which 6 were waited for; matrix products, arithmetic and copies ran while one was open for 6% of the time, Pallas kernels for 0%

commit v1 on v0

--- a/solution.py
+++ b/solution.py
@@ -39,7 +39,7 @@
     gram_local = lax.dot_general(
         item_factors, item_factors, (((0,), (0,)), ((), ())), preferred_element_type=jnp.float32
     )
-    gram = lax.psum(gram_local, ("blk", "grp"))
+    gram = lax.psum(lax.psum(gram_local, "blk"), "grp")
     pair_tiles = fetch_tiles(item_factors, item_tiles, pairs, tile, rank)
     live = jnp.sum(jnp.any(counts > 0, axis=(1, 2)).astype(jnp.int32))
     rounds = (live + span - 1) // span

time: 795 us -> 754 us (0.948)
  waiting for transfers between devices: 576 us -> 534 us
    psum x1, waiting for transfers between devices: 58.5 us -> 0.01 us  [body(): gram = lax.psum(lax.psum(gram_local, 'blk'), 'grp')]
    psum x1, waiting for transfers between devices: 106 us -> 122 us  [body(): pair_total, rhs_total = lax.psum((pair_part, rhs_part), 'grp')]
    unnamed x32 -> x30, local copies, waits for them, and re-layouts: 28.6 us -> 28.6 us
  transfers between devices with their start and end apart: 7 -> 7, of which waited for: 6 -> 5; matrix products, arithmetic and copies ran while one was open for 6% -> 6% of each run, Pallas kernels for 0% -> 0%
where the time goes in v1:
time: 754 us; the launch traced here: 746 us
  waiting for transfers between devices  534 us (71%)
  local copies, waits for them, and re-layouts  78.8 us (10%)
  matrix products  70.2 us (9%)
  blocking collectives  20.5 us (3%)
  other arithmetic  19.5 us (3%)
  between operations  15.6 us (2%)
    psum x3, waiting for transfers between devices, body(): image = gram_term(direction) + lax.psum(pair_part, 'grp')  307 us
    psum x1, waiting for transfers between devices, body(): pair_total, rhs_total = lax.psum((pair_part, rhs_part), 'grp')  122 us
    all_gather x1, waiting for transfers between devices, body(): whole = lax.all_gather(user_prior, 'grp', axis=0, tiled=True)  105 us
    unnamed x30, local copies, waits for them, and re-layouts  28.6 us
    dot_general x4, matrix products, one_round(): jnp.einsum('tb,bur->tur', selector, back, precision=lax.Precision.HIGHEST)  23.8 us
    dot_general x4, matrix products, gram_term(): jnp.dot(vectors, gram, precision=lax.Precision.HIGHEST) + REG * vectors  23.1 us
    all_to_all x1, blocking collectives, fetch_tiles(): lax.all_to_all(requests, ('blk', 'grp'), split_axis=0, concat_axis=0, til...  20.5 us
    while x5, local copies, waits for them, and re-layouts, accumulate(): totals = lax.fori_loop(0, rounds, one_round, start_state)  16.4 us
  transfers between devices with their start and end apart: 7, of which 5 were waited for; matrix products, arithmetic and copies ran while one was open for 6% of the time, Pallas kernels for 0%

profile of v1, /device:TPU:0, one launch (start us, length us, event | category | flops | bytes accessed | tf_op | source)
XLA Modules:
  0.0 746.4 jit_solution(12308487806630761720)
XLA Ops:
  15.3 20.5 %all_to_all.14 = s32[128,1,2]{2,1,0:T(1,128)S(1)} all-to-all(s32[128,1,2]{2,1,0:T(1,128)S(1)} %copy.108), channel_id=1, replica_groups=mesh['blk'=8,'grp'=16] {'blk','grp'}, dimensions={0} | all-to-all | bytes 2048 | tf_op jit(solution)/shard_map/all_to_all | solution.py:22
  36.4 8.4 %gather_fusion.4 = bf16[256,128,128]{2,1,0:T(8,128)(2,1)} fusion(bf16[32,128,128]{2,1,0:T(8,128)(2,1)S(1)} %bitcast.108, s32[1024]{0:T(1024)S(1)} %pad_clamp_fusion.4), kind=kCustom, calls=%fused_computation.4 | custom fusion | bytes 16778240 | tf_op jit(solution)/shard_map/jit(_take)/gather | solution.py:24
  44.8 7.4 select_select_fusion
  52.2 6.1 all-to-all-start.1
  60.9 105.2 %all-gather.2.cloned.1.call-done = f32[4096,128]{0,1:T(8,128)} async-done(((f32[256,128]{0,1:T(8,128)}), f32[4096,128]{0,1:T(8,128)}) %all-gather.2.cloned.1.call-update) | async-done | bytes 2097168 | tf_op jit(solution)/shard_map/all_gather | solution.py:88
  176.7 18.2 %while.46 = (s32[]{:T(128)}, f32[32,128,128]{2,0,1:T(8,128)}, f32[32,128,128]{2,0,1:T(8,128)}, s32[]{:T(128)}, s32[64]{0:T(128)S(1)}, /*index=5*/s32[64,128,128]...) while((s32[]{:T(128)}, f32[32,128,128]{2,0,1:T(8,128)}, ...), condition=%wide.region_5.7_spmd.clone, body=%wide.region_4.6_spmd.clone.sunk | while | flops 812125440 | bytes 44048128 | solution.py:79
  183.1 6.1 fusion.187
  189.6 5.4 fusion.189
  198.4 4.6 copy.165
  211.3 121.8 %all-reduce.15.cloned.1.call-done = (f32[4096,128]{0,1:T(8,128)}, f32[4096,128]{0,1:T(8,128)}, f32[128,128]{1,0:T(8,128)}) async-done(((f32[4096,128]{0,1:T(8,128)}, f32[4096,128]{0,1:T(8,128)}, f32[128,128]{1,0:T(8,128)}), (f32[4096,128]{0,1:T(8,128)}, f32[4096,128]{0,1:T(8,128)}, f32[128,128]{1,0:T(8,128)})) %all-reduce.15.cloned.1.call-update) | async-done | bytes 4259856 | tf_op jit(solution)/shard_map/psum | solution.py:92
  333.1 7.0 fusion.133
  343.0 12.0 %while.47 = (s32[]{:T(128)}, f32[32,128,128]{2,0,1:T(8,128)}, s32[]{:T(128)}, s32[64]{0:T(128)S(1)}, s32[64,128,128]{2,1,0:T(8,128)}, /*index=5*/bf16[32,128,128...) while((s32[]{:T(128)}, f32[32,128,128]{2,0,1:T(8,128)}, ...), condition=%wide.region_12.14_spmd.clone, body=%wide.region_11.13_spmd.clone.sunk | while | flops 472910112 | bytes 15735391 | solution.py:79
  349.2 5.9 fusion.196
  363.3 102.4 %all-reduce.9.cloned.1.call-done = f32[4096,128]{0,1:T(8,128)} async-done(((f32[4096,128]{0,1:T(8,128)}), f32[4096,128]{0,1:T(8,128)}) %all-reduce.9.cloned.1.call-update) | async-done | bytes 2097168 | tf_op jit(solution)/shard_map/psum | solution.py:101
  465.8 5.5 multiply_reduce_fusion.3
  476.6 12.1 %while.48 = (s32[]{:T(128)}, f32[32,128,128]{2,0,1:T(8,128)}, s32[]{:T(128)}, s32[64]{0:T(128)S(1)}, s32[64,128,128]{2,1,0:T(8,128)}, /*index=5*/bf16[32,128,128...) while((s32[]{:T(128)}, f32[32,128,128]{2,0,1:T(8,128)}, ...), condition=%wide.region_17.19_spmd.clone, body=%wide.region_16.18_spmd.clone.sunk | while | flops 472910112 | bytes 15735391 | solution.py:79
  482.8 5.9 fusion.203
  492.1 4.6 copy.163
  497.2 102.2 %all-reduce.11.cloned.1.call-done = f32[4096,128]{0,1:T(8,128)} async-done(((f32[4096,128]{0,1:T(8,128)}), f32[4096,128]{0,1:T(8,128)}) %all-reduce.11.cloned.1.call-update) | async-done | bytes 2097168 | tf_op jit(solution)/shard_map/psum | solution.py:101
  599.4 5.3 multiply_reduce_fusion.1
  611.2 12.3 %while.49 = (s32[]{:T(128)}, f32[32,128,128]{2,0,1:T(8,128)}, s32[]{:T(128)}, s32[64]{0:T(128)S(1)}, s32[64,128,128]{2,1,0:T(8,128)}, /*index=5*/bf16[32,128,128...) while((s32[]{:T(128)}, f32[32,128,128]{2,0,1:T(8,128)}, ...), condition=%wide.region_22.24_spmd.clone, body=%wide.region_21.23_spmd.clone.sunk | while | flops 472910112 | bytes 15735391 | solution.py:79
  617.3 5.9 fusion.210
  629.3 102.5 %all-reduce.13.cloned.1.call-done = f32[4096,128]{0,1:T(8,128)} async-done(((f32[4096,128]{0,1:T(8,128)}), f32[4096,128]{0,1:T(8,128)}) %all-reduce.13.cloned.1.call-update) | async-done | bytes 2097168 | tf_op jit(solution)/shard_map/psum | solution.py:101
  731.8 5.2 fusion.123
  (107 shorter events, 92.5 us)
Async XLA Ops:
  7.4 29.0 %copy-start = (bf16[4096,128]{1,0:T(8,128)(2,1)S(1)}, bf16[4096,128]{1,0:T(8,128)(2,1)}, u32[]{:S(2)}) copy-start(bf16[4096,128]{1,0:T(8,128)(2,1)} %param.16) | copy-start | bytes 3145732
  7.4 3.5 copy-start.10
  52.2 6.1 copy-start.9
  52.2 117.0 %all-to-all-start.1 = ((bf16[128,2,128,128]{3,2,1,0:T(8,128)(2,1)}), bf16[128,2,128,128]{3,2,1,0:T(8,128)(2,1)}, u32[]{:S(2)}, u32[]{:S(2)}) async-start(bf16[128,2,128,128]{3,2,1,0:T(8,128)(2,1)} %select_select_fusion), calls=%async_computation.1 | async-start | bytes 16777216 | tf_op jit(solution)/shard_map/all_to_all | solution.py:26
  58.3 107.8 %all-gather.2.cloned.1.call-start = ((), (), s32[]{:S(2)}) async-start(), calls=%async_computation.2 | async-start | bytes 2228224 | tf_op jit(solution)/shard_map/all_gather | solution.py:88
  59.1 151.9 %all-reduce.7.cloned.1.call-start = ((), (), s32[]{:S(2)}) async-start(), calls=%async_computation.3 | async-start | bytes 131072 | tf_op jit(solution)/shard_map/psum | solution.py:42
  60.3 272.8 %all-reduce.15.cloned.1.call-start = ((), (), s32[]{:S(2)}) async-start(), calls=%async_computation.7 | async-start | bytes 8519680 | tf_op jit(solution)/shard_map/psum | solution.py:92
  173.5 3.2 copy-start.8
  183.1 6.1 copy-start.2
  211.0 254.7 %all-reduce.9.cloned.1.call-start = ((), (), s32[]{:S(2)}) async-start(), calls=%async_computation.4 | async-start | bytes 4194304 | tf_op jit(solution)/shard_map/psum | solution.py:101
  363.0 102.7 %copy-start.7 = (f32[128,128]{1,0:T(8,128)S(1)}, f32[128,128]{1,0:T(8,128)}, u32[]{:S(2)}) copy-start(f32[128,128]{1,0:T(8,128)} %get-tuple-element.495) | copy-start | bytes 196612
  363.0 236.4 %all-reduce.11.cloned.1.call-start = ((), (), s32[]{:S(2)}) async-start(), calls=%async_computation.5 | async-start | bytes 4194304 | tf_op jit(solution)/shard_map/psum | solution.py:101
  465.8 5.5 copy-start.3
  471.7 2.0 copy-start.4
  496.7 235.1 %all-reduce.13.cloned.1.call-start = ((), (), s32[]{:S(2)}) async-start(), calls=%async_computation.6 | async-start | bytes 4194304 | tf_op jit(solution)/shard_map/psum | solution.py:101
  599.4 5.4 copy-start.5
  604.8 1.6 copy-start.6
  731.8 7.2 copy-start.1
Sparse Core Ops, SparseCore 0:
  61.2 104.8 all-gather.1
  211.2 121.8 all-reduce.14
  363.2 102.5 all-reduce.8
  496.9 102.5 all-reduce.10
  629.3 102.5 all-reduce.12
Sparse Core Ops, SparseCore 1:
  61.9 111.2 all-reduce.6
